TPU v7x, 256 devices: a whole 4x4x8 slice. The times are simulated.
256 devices in a mesh: seq: 32 (over z, x), feat: 8 (over y, core).
Axes of the slice: x: 4, y: 4, z: 8, core: 2. Of those that a mesh axis runs over, the one named last changes fastest.
Arguments:
- teacher_states: bfloat16 [4, 32768, 3584], P(None, 'seq', 'feat')
- student_states: bfloat16 [32768, 2304], P('seq'), may hold values from -6 to 6
- projection: bfloat16 [4, 2304, 3584], P(None, 'seq', 'feat'), may hold values from -0.125 to 0.125
- layer_pick: int32 [4], replicated, may hold values from 0 to 3, each once
- validity: int32 [32768], P('seq'), may hold values from 0 to 1, as said below
Outputs:
- whitened_error: bfloat16 [4, 32768, 3584], P(None, 'seq', 'feat')
- total_loss: float32 [], replicated
Inputs may be any that keep to these rules, and one draw needn't show every extreme that they name: `validity`: the positions form 2 sequences of 16384 positions each; in each sequence a prefix of 4096 positions or more is 1 and the rest is 0.
All inputs are finite; a program needn't handle non-finite values.
Results may differ from a plain program's by a relative error of at most 0.00045.
Values may be sent and summed in bfloat16 or wider, within the bound.
No kernel may reach another device: no remote copies, remote signals or barrier semaphores. Data moves between devices by JAX's collectives and lax.ppermute only.
A program may use at most 64 MiB of HBM per device.

v0:
```python
import functools
import jax
import jax.numpy as jnp
from jax import lax
from jax.sharding import Mesh
from jax.sharding import PartitionSpec as P

D = 3584
LAYERS = 4
SEQ = ("seq_0", "seq_1")
SEQ_FEAT = ("seq_0", "seq_1", "feat_0", "feat_1")
FEAT = ("feat_0", "feat_1")
epsilon = 1e-05


def all_in_one(value, axis):
    leaves = jax.tree.leaves(value)
    sequence = sorted(range(len(leaves)), key=lambda k: -leaves[k].size)
    width = (1, *leaves[sequence[0]].shape)[-1]
    lines = [
        jnp.pad(leaves[k].reshape(-1), (0, -leaves[k].size % width)).reshape(-1, width)
        for k in sequence
    ]
    both, at, found = (lax.all_gather(jnp.concatenate(lines), axis), 0, {})
    for k, line in zip(sequence, lines):
        slab = both[:, at : at + len(line)].reshape(len(both), -1)
        found[k] = slab[:, : leaves[k].size].reshape(-1, *leaves[k].shape)
        at += len(line)
    numbers = iter(range(len(leaves)))
    return jax.tree.map(lambda _: found[next(numbers)], value)


def combined_by_axis(value, axes, combine):
    for axis in axes:
        pieces = all_in_one(value, axis)
        value = jax.tree.map(lambda part: part[0], pieces)
        for k in range(1, lax.axis_size(axis)):
            value = combine(value, jax.tree.map(lambda part: part[k], pieces))
    return value


def over_axes(value, axes):
    return functools.reduce(lax.psum, axes, value)


def combine_moments(former, latter):
    first_count, first_mean, first_spread = former
    second_count, second_mean, second_spread = latter
    joined = first_count + second_count
    share = second_count / jnp.maximum(joined, 1.0)
    delta = second_mean - first_mean
    return (
        joined,
        first_mean + delta * share,
        first_spread + second_spread + delta * delta * first_count * share,
    )


def shards(teacher_states, student_states, projection, layer_pick, validity):
    all_weights = lax.all_gather(projection, SEQ, axis=1, tiled=True)
    weighting = validity.astype(jnp.float32)
    local_count = jnp.sum(weighting)
    chosen = jnp.take(teacher_states, layer_pick, axis=0).astype(jnp.float32)
    masked = weighting[None, :, None]
    local_sums = jnp.sum(chosen * masked, axis=1)
    local_mean = local_sums / jnp.maximum(local_count, 1.0)
    local_centred = chosen - local_mean[:, None, :]
    local_spread = jnp.sum(masked * local_centred * local_centred, axis=1)
    counted, average, spread = combined_by_axis(
        (local_count, local_mean, local_spread), SEQ, combine_moments
    )
    variance = spread / counted
    centred = chosen - average[:, None, :]
    target = centred / jnp.sqrt(variance + epsilon)[:, None, :]
    predicted = jnp.einsum(
        "tr,lrd->ltd", student_states, all_weights, preferred_element_type=jnp.float32
    )
    residual = predicted - target
    whitened_error = (masked * residual).astype(jnp.bfloat16)
    partial_value = jnp.sum(masked * residual * residual)
    squared_total = over_axes(partial_value, SEQ_FEAT)
    total_loss = squared_total / (counted * D * LAYERS)
    return (whitened_error, total_loss)


def solution(mesh):
    torus = Mesh(mesh.devices.reshape(8, 4, 4, 2), ("seq_0", "seq_1", "feat_0", "feat_1"))
    in_specs = (P(None, SEQ, FEAT), P(SEQ, None), P(None, SEQ, FEAT), P(), P(SEQ))
    out_specs = (P(None, SEQ, FEAT), P())
    return jax.shard_map(
        shards, mesh=torus, in_specs=in_specs, out_specs=out_specs, check_vma=False
    )
```

profile of v0, /device:TPU:1, one launch (start us, length us, event | category | flops | bytes accessed | tf_op | source)
XLA Modules:
  0.0 185.9 jit_solution(15718595818975984317)
XLA Ops:
  7.2 0.0 copy-start.1
  7.2 0.0 copy-start.2
  7.2 0.0 all-gather.6.cloned.1.call-start
  7.2 0.7 all-gather.6.cloned.1.call-update
  7.9 0.7 convert_element_type.12
  8.6 0.7 compare_select_fusion
  9.3 4.7 %gather_fusion = bf16[4,1024,448]{1,2,0:T(8,128)(2,1)} fusion(bf16[4,1024,448]{1,2,0:T(8,128)(2,1)} %param.5, s32[1024]{0:T(1024)S(1)} %pad_clamp_fusion), kind=kCustom, calls=%fused_computation | custom fusion | bytes 7340048 | tf_op jit(solution)/shard_map/jit(_take)/gather | solution.py:63
  13.9 0.0 copy-done.1
  13.9 0.6 convert_reduce_fusion
  15.2 0.0 copy-start
  15.2 0.8 pad.7
  16.0 0.0 copy-done.2
  16.0 3.3 %fusion.1 = f32[4,448]{1,0:T(4,128)S(1)} fusion(f32[1024]{0:T(1024)S(1)} %convert_element_type.12, bf16[4,1024,448]{1,2,0:T(8,128)(2,1)} %gather_fusion, pred[4]{0:T(512)(128)(4,1)S(1)} %compare_and_fusion), kind=kLoop, calls=%fused_computation.8 | loop fusion | flops 7338240 | bytes 3681284 | tf_op jit(solution)/shard_map/reduce_sum | solution.py:65
  19.4 0.0 copy-done
  19.4 1.8 fusion.4
  21.2 24.3 %all-gather.2 = f32[8,9,448]{2,1,0:T(8,128)S(1)} all-gather(f32[1,9,448]{2,1,0:T(8,128)S(1)} %maximum_bitcast_fusion), channel_id=2, replica_groups=mesh['seq_0'=8,'seq_1'=4,'feat_0'=4,'feat_1'=2] {'seq_0'}, dimensions={0}, use_global_device_ids=true | all-gather | bytes 145152 | tf_op jit(solution)/shard_map/all_gather | solution.py:24
  45.6 0.6 fusion.40
  55.8 0.7 fusion.20
  56.5 9.7 %all-gather.3 = f32[4,9,448]{2,1,0:T(8,128)S(1)} all-gather(f32[1,9,448]{2,1,0:T(8,128)S(1)} %maximum_bitcast_fusion.1), channel_id=3, replica_groups=mesh['seq_0'=8,'seq_1'=4,'feat_0'=4,'feat_1'=2] {'seq_1'}, dimensions={0}, use_global_device_ids=true | all-gather | bytes 80640 | tf_op jit(solution)/shard_map/all_gather | solution.py:24
  66.2 0.6 fusion.41
  71.3 0.7 multiply_add_fusion
  72.0 46.2 %all-gather.6.cloned.1.call-done = bf16[4,2304,448]{2,1,0:T(8,128)(2,1)} async-done(((bf16[4,72,448]{2,1,0:T(8,128)(2,1)}), bf16[4,2304,448]{2,1,0:T(8,128)(2,1)}) %all-gather.6.cloned.1.call-update) | async-done | bytes 8257552 | tf_op jit(solution)/shard_map/all_gather | solution.py:60
  118.2 19.1 %fusion = (f32[]{:T(128)}, bf16[4,1024,448]{1,2,0:T(8,128)(2,1)}) fusion(f32[1024]{0:T(1024)S(1)} %convert_element_type.12, f32[4,448]{1,0:T(4,128)S(1)} %get-tuple-element.7, f32[4,448]{1,0:T(4,128)S(1)} %get-tuple-element.6, bf16[4,1024,448]{1,2,0:T(8,128)(2,1)} %gather_fusion, pred[4]{0:T(512)(128)(4,1)S(1)} %compare_and_fusion, ...), kind=kOutput, calls=%fused_computation.7 | convolution fusion | flops 8472231936 | bytes 20334600 | tf_op jit(solution)/shard_map/tr,lrd->ltd/dot_general | solution.py:75
  137.3 13.0 %psum.28 = f32[]{:T(128)} all-reduce(f32[]{:T(128)} %get-tuple-element.4), channel_id=1, replica_groups=mesh['seq_0'=8,'seq_1'=4,'feat_0'=4,'feat_1'=2] {'seq_0'}, use_global_device_ids=true, to_apply=%region_4.5 | all-reduce | flops 1 | bytes 8 | tf_op jit(solution)/shard_map/psum | solution.py:43
  150.3 6.6 %psum.29 = f32[]{:T(128)} all-reduce(f32[]{:T(128)} %psum.28), channel_id=1, replica_groups=mesh['seq_0'=8,'seq_1'=4,'feat_0'=4,'feat_1'=2] {'seq_1'}, use_global_device_ids=true, to_apply=%region_5.6 | all-reduce | flops 1 | bytes 8 | tf_op jit(solution)/shard_map/psum | solution.py:43
  156.9 8.8 %psum.30 = f32[]{:T(128)} all-reduce(f32[]{:T(128)} %psum.29), channel_id=1, replica_groups=mesh['seq_0'=8,'seq_1'=4,'feat_0'=4,'feat_1'=2] {'feat_0'}, use_global_device_ids=true, to_apply=%region_6.7 | all-reduce | flops 1 | bytes 8 | tf_op jit(solution)/shard_map/psum | solution.py:43
  165.7 11.6 %psum.31 = f32[]{:T(128)} all-reduce(f32[]{:T(128)} %psum.30), channel_id=1, replica_groups=mesh['seq_0'=8,'seq_1'=4,'feat_0'=4,'feat_1'=2] {'feat_1'}, use_global_device_ids=true, to_apply=%region_7.8 | all-reduce | flops 1 | bytes 8 | tf_op jit(solution)/shard_map/psum | solution.py:43
  (11 shorter events, 0.1 us)
Async XLA Ops:
  7.2 6.8 %copy-start.1 = (s32[1024]{0:T(1024)S(1)}, s32[1024]{0:T(1024)}, u32[]{:S(2)}) copy-start(s32[1024]{0:T(1024)} %param.9) | copy-start | bytes 12292
  7.2 8.8 %copy-start.2 = (s32[4]{0:T(128)S(1)}, s32[4]{0:T(128)}, u32[]{:S(2)}) copy-start(s32[4]{0:T(128)} %param.8) | copy-start | bytes 52
  7.2 111.0 %all-gather.6.cloned.1.call-start = ((), (), s32[]{:S(2)}) async-start(), calls=%async_computation | async-start | bytes 9732096 | tf_op jit(solution)/shard_map/all_gather | solution.py:60
  15.2 4.2 %copy-start = (bf16[4,1024,448]{1,2,0:T(8,128)(2,1)S(1)}, bf16[4,1024,448]{1,2,0:T(8,128)(2,1)}, u32[]{:S(2)}) copy-start(bf16[4,1024,448]{1,2,0:T(8,128)(2,1)} %gather_fusion) | copy-start | bytes 11010052
Sparse Core Ops, SparseCore 0:
  10.6 107.5 all-gather.5
where the time goes:
time: 186 us
  blocking collectives  74.1 us (40%)
  waiting for transfers between devices  46.9 us (25%)
  between operations  30.6 us (16%)
  matrix products  19.1 us (10%)
  other arithmetic  8.52 us (5%)
  local copies, waits for them, and re-layouts  6.71 us (4%)
    all_gather x1, waiting for transfers between devices, shards(): all_weights = lax.all_gather(projection, SEQ, axis=1, tiled=True)  46.2 us
    psum x4, blocking collectives, over_axes(): return functools.reduce(lax.psum, axes, value)  40 us
    all_gather x2, blocking collectives, all_in_one(): both, at, found = (lax.all_gather(jnp.concatenate(lines), axis), 0, {})  34 us
    dot_general x1, matrix products, shards(): jnp.einsum('tr,lrd->ltd', student_states, all_weights, preferred_element_...  19.1 us
    gather x1, local copies, waits for them, and re-layouts, shards(): chosen = jnp.take(teacher_states, layer_pick, axis=0).astype(jnp.float32)  4.65 us
  transfers between devices with their start and end apart: 1, of which 1 were waited for; matrix products, arithmetic and copies ran while one was open for 8% of the time, Pallas kernels for 0%

commit v1 on v0

--- a/solution.py
+++ b/solution.py
@@ -57,7 +57,15 @@
 
 
 def shards(teacher_states, student_states, projection, layer_pick, validity):
-    all_weights = lax.all_gather(projection, SEQ, axis=1, tiled=True)
+    all_weights = jnp.concatenate(
+        jax.lax.all_to_all(
+            jnp.stack([projection for _ in range(jax.lax.axis_size(SEQ))], axis=0),
+            axis_name=SEQ,
+            concat_axis=0,
+            split_axis=0,
+        ),
+        1,
+    )
     weighting = validity.astype(jnp.float32)
     local_count = jnp.sum(weighting)
     chosen = jnp.take(teacher_states, layer_pick, axis=0).astype(jnp.float32)

time: 186 us -> 360 us (1.94)
  blocking collectives: 74.1 us -> 282 us
  waiting for transfers between devices: 46.9 us -> 0.01 us
  between operations: 30.6 us -> 16.8 us
  local copies, waits for them, and re-layouts: 6.71 us -> 20.5 us
  starting transfers between devices: 0.04 us -> 12.1 us
    all_gather x2, blocking collectives: 34 us -> 232 us  [all_in_one(): both, at, found = (lax.all_gather(jnp.concatenate(lines), axis), 0, {})]
    all_gather x1 -> x0, waiting for transfers between devices: 46.2 us -> none  [shards(): all_weights = lax.all_gather(projection, SEQ, axis=1, tiled=True)]
    all_to_all x0 -> x1, starting transfers between devices: none -> 12.1 us  [shards(): jax.lax.all_to_all(jnp.stack([projection for _ in range(jax.lax.axis_size...]
    psum x4, blocking collectives: 40 us -> 49.6 us  [over_axes(): return functools.reduce(lax.psum, axes, value)]
    reshape x0 -> x1, local copies, waits for them, and re-layouts: none -> 8.23 us  [shards(): jnp.concatenate(jax.lax.all_to_all(jnp.stack([projection for _ in range(j...]
    another operation x0 -> x1, local copies, waits for them, and re-layouts: none -> 5.72 us  [shards(): jnp.stack([projection for _ in range(jax.lax.axis_size(SEQ))], axis=0)]
  transfers between devices with their start and end apart: 1 -> 1, of which waited for: 1 -> 0; matrix products, arithmetic and copies ran while one was open for 8% -> 4% of each run, Pallas kernels for 0% -> 0%
where the time goes in v1:
time: 360 us; the launch traced here: 359 us
  blocking collectives  282 us (78%)
  local copies, waits for them, and re-layouts  20.5 us (6%)
  matrix products  19.1 us (5%)
  between operations  16.8 us (5%)
  starting transfers between devices  12.1 us (3%)
  other arithmetic  8.43 us (2%)
    all_gather x2, blocking collectives, all_in_one(): both, at, found = (lax.all_gather(jnp.concatenate(lines), axis), 0, {})  232 us
    psum x4, blocking collectives, over_axes(): return functools.reduce(lax.psum, axes, value)  49.6 us
    dot_general x1, matrix products, shards(): jnp.einsum('tr,lrd->ltd', student_states, all_weights, preferred_element_...  19.1 us
    all_to_all x1, starting transfers between devices, shards(): jax.lax.all_to_all(jnp.stack([projection for _ in range(jax.lax.axis_size...  12.1 us
    reshape x1, local copies, waits for them, and re-layouts, shards(): jnp.concatenate(jax.lax.all_to_all(jnp.stack([projection for _ in range(j...  8.23 us
  transfers between devices with their start and end apart: 1, of which 0 were waited for; matrix products, arithmetic and copies ran while one was open for 4% of the time, Pallas kernels for 0%

profile of v1, /device:TPU:1, one launch (start us, length us, event | category | flops | bytes accessed | tf_op | source)
XLA Modules:
  0.0 358.9 jit_solution(16790951285787530610)
XLA Ops:
  0.6 5.7 %stack.2 = bf16[32,4,72,448]{3,2,1,0:T(8,128)(2,1)} broadcast(bf16[4,72,448]{2,1,0:T(8,128)(2,1)} %param.7), dimensions={1,2,3} | broadcast | bytes 8515584 | tf_op jit(solution)/shard_map/stack | solution.py:62
  6.3 0.0 copy-start
  6.3 0.0 copy-start.1
  6.3 12.1 %all-to-all-start = ((bf16[32,4,72,448]{3,2,1,0:T(8,128)(2,1)}), bf16[32,4,72,448]{3,2,1,0:T(8,128)(2,1)}, u32[]{:S(2)}, u32[]{:S(2)}) async-start(bf16[32,4,72,448]{3,2,1,0:T(8,128)(2,1)} %stack.2), calls=%async_computation | async-start | bytes 18874368 | tf_op jit(solution)/shard_map/all_to_all | solution.py:61
  18.5 0.0 copy-done
  18.5 0.6 convert_reduce_fusion
  19.7 0.7 pad.7
  20.4 0.0 copy-done.1
  20.4 4.7 %gather_fusion = bf16[4,1024,448]{1,2,0:T(8,128)(2,1)} fusion(bf16[4,1024,448]{1,2,0:T(8,128)(2,1)} %param.5, s32[1024]{0:T(1024)S(1)} %pad_clamp_fusion), kind=kCustom, calls=%fused_computation | custom fusion | bytes 7340048 | tf_op jit(solution)/shard_map/jit(_take)/gather | solution.py:71
  25.1 3.1 fusion.1
  28.2 3.3 fusion.4
  31.6 212.5 %all-gather.2 = f32[8,9,448]{2,1,0:T(8,128)S(1)} all-gather(f32[1,9,448]{2,1,0:T(8,128)S(1)} %maximum_bitcast_fusion), channel_id=2, replica_groups=mesh['seq_0'=8,'seq_1'=4,'feat_0'=4,'feat_1'=2] {'seq_0'}, dimensions={0}, use_global_device_ids=true | all-gather | bytes 145152 | tf_op jit(solution)/shard_map/all_gather | solution.py:24
  244.1 0.6 fusion.40
  254.2 0.7 fusion.20
  254.9 19.8 %all-gather.3 = f32[4,9,448]{2,1,0:T(8,128)S(1)} all-gather(f32[1,9,448]{2,1,0:T(8,128)S(1)} %maximum_bitcast_fusion.1), channel_id=3, replica_groups=mesh['seq_0'=8,'seq_1'=4,'feat_0'=4,'feat_1'=2] {'seq_1'}, dimensions={0}, use_global_device_ids=true | all-gather | bytes 80640 | tf_op jit(solution)/shard_map/all_gather | solution.py:24
  274.7 0.6 fusion.41
  279.5 0.6 multiply_add_fusion
  280.2 0.0 all-to-all-done
  280.2 8.2 %copy.9 = bf16[4,32,72,448]{3,2,1,0:T(8,128)(2,1)} copy(bf16[4,32,72,448]{3,2,0,1:T(8,128)(2,1)} %bitcast) | data formatting | bytes 16515072 | tf_op jit(solution)/shard_map/reshape | solution.py:60
  288.4 19.1 %fusion = (f32[]{:T(128)}, bf16[4,1024,448]{1,2,0:T(8,128)(2,1)}) fusion(f32[1024]{0:T(1024)S(1)} %convert_element_type.12, f32[4,448]{1,0:T(4,128)S(1)} %get-tuple-element.7, f32[4,448]{1,0:T(4,128)S(1)} %get-tuple-element.6, bf16[4,1024,448]{1,2,0:T(8,128)(2,1)} %gather_fusion, pred[4]{0:T(512)(128)(4,1)S(1)} %compare_and_fusion, ...), kind=kOutput, calls=%fused_computation.7 | convolution fusion | flops 8472231936 | bytes 20334600 | tf_op jit(solution)/shard_map/tr,lrd->ltd/dot_general | solution.py:83
  307.5 11.3 %psum.28 = f32[]{:T(128)} all-reduce(f32[]{:T(128)} %get-tuple-element.4), channel_id=1, replica_groups=mesh['seq_0'=8,'seq_1'=4,'feat_0'=4,'feat_1'=2] {'seq_0'}, use_global_device_ids=true, to_apply=%region_4.5 | all-reduce | flops 1 | bytes 8 | tf_op jit(solution)/shard_map/psum | solution.py:43
  318.8 9.3 %psum.29 = f32[]{:T(128)} all-reduce(f32[]{:T(128)} %psum.28), channel_id=1, replica_groups=mesh['seq_0'=8,'seq_1'=4,'feat_0'=4,'feat_1'=2] {'seq_1'}, use_global_device_ids=true, to_apply=%region_5.6 | all-reduce | flops 1 | bytes 8 | tf_op jit(solution)/shard_map/psum | solution.py:43
  328.0 9.3 %psum.30 = f32[]{:T(128)} all-reduce(f32[]{:T(128)} %psum.29), channel_id=1, replica_groups=mesh['seq_0'=8,'seq_1'=4,'feat_0'=4,'feat_1'=2] {'feat_0'}, use_global_device_ids=true, to_apply=%region_6.7 | all-reduce | flops 1 | bytes 8 | tf_op jit(solution)/shard_map/psum | solution.py:43
  337.4 19.7 %psum.31 = f32[]{:T(128)} all-reduce(f32[]{:T(128)} %psum.30), channel_id=1, replica_groups=mesh['seq_0'=8,'seq_1'=4,'feat_0'=4,'feat_1'=2] {'feat_1'}, use_global_device_ids=true, to_apply=%region_7.8 | all-reduce | flops 1 | bytes 8 | tf_op jit(solution)/shard_map/psum | solution.py:43
  (13 shorter events, 0.1 us)
Async XLA Ops:
  6.3 12.1 %copy-start = (s32[1024]{0:T(1024)S(1)}, s32[1024]{0:T(1024)}, u32[]{:S(2)}) copy-start(s32[1024]{0:T(1024)} %param.9) | copy-start | bytes 12292
  6.3 14.1 %copy-start.1 = (s32[4]{0:T(128)S(1)}, s32[4]{0:T(128)}, u32[]{:S(2)}) copy-start(s32[4]{0:T(128)} %param.8) | copy-start | bytes 52
  6.3 273.8 %all-to-all-start = ((bf16[32,4,72,448]{3,2,1,0:T(8,128)(2,1)}), bf16[32,4,72,448]{3,2,1,0:T(8,128)(2,1)}, u32[]{:S(2)}, u32[]{:S(2)}) async-start(bf16[32,4,72,448]{3,2,1,0:T(8,128)(2,1)} %stack.2), calls=%async_computation | async-start | bytes 18874368 | tf_op jit(solution)/shard_map/all_to_all | solution.py:61
